TPU v7x, 32 devices: a whole 2x2x4 slice. The times are simulated.
32 devices in a mesh: dp: 16 (over z, y, x), expert: 2 (over core).
Axes of the slice: x: 2, y: 2, z: 4, core: 2. Of those that a mesh axis runs over, the one named last changes fastest.
Arguments:
- latents: bfloat16 [4096, 2048], P('dp', 'expert'), as said below
- cotangent: bfloat16 [4096, 2048], P('dp', 'expert'), may hold values from -6 to 6
- routes: int32 [4096, 2], P('dp'), may hold values from 0 to 15, all different within a row; in each aligned block of 256 rows (0 to 255, 256 to 511, ...) at most 48 rows name the same one
- router_w: float32 [2048, 16], P('expert'), may hold values from -1 to 1
- mod_shift: bfloat16 [1, 2048], P(None, 'expert'), may hold values from -3 to 3
- mod_scale: bfloat16 [1, 2048], P(None, 'expert'), may hold values from -1.5 to 2.5
- mod_gate: bfloat16 [1, 2048], P(None, 'expert'), may hold values from -4 to 4
- gate_w: bfloat16 [16, 2048, 1024], P('dp', None, 'expert'), may hold values from -0.125 to 0.125
- up_w: bfloat16 [16, 2048, 1024], P('dp', None, 'expert'), may hold values from -0.125 to 0.125
- down_w: bfloat16 [16, 1024, 2048], P('dp', 'expert'), may hold values from -0.1875 to 0.1875
Outputs:
- latent_gradient: bfloat16 [4096, 2048], P('dp', 'expert')
- grad_gate_w: bfloat16 [16, 2048, 1024], P('dp', None, 'expert')
- grad_up_w: bfloat16 [16, 2048, 1024], P('dp', None, 'expert')
- grad_down_w: bfloat16 [16, 1024, 2048], P('dp', 'expert')
- grad_router: float32 [2048, 16], P('expert')
Inputs may be any that keep to these rules, and one draw needn't show every extreme that they name: `routes`: the two experts of a token differ. Among the 256 tokens of one aligned block (the tokens of one index of dp), no expert is named more than 48 times, a bound that some block reaches. Columns and rows of latents have unlike scales.
All inputs are finite; a program needn't handle non-finite values.
Results may differ from a plain program's by a relative error of at most 0.008.
Values may be sent and summed in bfloat16 or wider, within the bound.
No kernel may reach another device: no remote copies, remote signals or barrier semaphores. Data moves between devices by JAX's collectives and lax.ppermute only.
A program may use at most 128 MiB of HBM per device.

v0:
```python
import jax
import jax.numpy as jnp
from jax import lax
from jax.sharding import PartitionSpec as P

SEQ = 4096
norm_eps = 1e-06


def slot_targets(routes, experts, capacity):
    flat_routes = routes.reshape(-1)
    expert_ids = jnp.arange(experts, dtype=jnp.int32)
    onehot = (flat_routes[:, None] == expert_ids[None, :]).astype(jnp.int32)
    rank_run = jnp.cumsum(onehot, axis=0) - 1
    return flat_routes * capacity + jnp.sum(onehot * rank_run, axis=1)


def selected_row(table, sample_index):
    return lax.dynamic_slice_in_dim(table, sample_index, 1, 0).astype(jnp.float32)


def owner_view(arrived, groups, local):
    shaped = arrived.reshape((groups, local) + arrived.shape[1:])
    shaped = jnp.swapaxes(shaped, 0, 1)
    return shaped.reshape((local, groups * arrived.shape[1]) + arrived.shape[2:])


def sender_view(outgoing, groups):
    local = outgoing.shape[0]
    capacity = outgoing.shape[1] // groups
    shaped = outgoing.reshape((local, groups, capacity) + outgoing.shape[2:])
    shaped = jnp.swapaxes(shaped, 0, 1)
    return shaped.reshape((groups * local, capacity) + outgoing.shape[2:])


def route_weights(logits, routes, experts):
    chances = jax.nn.sigmoid(logits)
    expert_ids = jnp.arange(experts, dtype=jnp.int32)
    hits = routes[:, :, None] == expert_ids[None, None, :]
    picked = jnp.sum(jnp.where(hits, chances[:, None, :], 0.0), axis=2)
    pick_sum = jnp.sum(picked, axis=1, keepdims=True)
    return (hits, picked, pick_sum, picked / pick_sum)


def fill_slots(rows_b, scaled_dy, weights_b, targets, slot_count):
    width_here = rows_b.shape[1]
    send_x = (
        jnp.zeros((slot_count, width_here), jnp.bfloat16)
        .at[targets]
        .set(jnp.repeat(rows_b, 2, axis=0))
    )
    send_z = (
        jnp.zeros((slot_count, width_here), jnp.bfloat16)
        .at[targets]
        .set(jnp.repeat(scaled_dy, 2, axis=0))
    )
    send_w = jnp.zeros((slot_count,), jnp.bfloat16).at[targets].set(weights_b.reshape(-1))
    return (send_x, send_z, send_w)


def expert_grads(gate_lin, up_lin, down_back, slot_w):
    gate_sig = jax.nn.sigmoid(gate_lin)
    gate_act = gate_lin * gate_sig
    hidden = gate_act * up_lin
    slot_score = jnp.sum(hidden * down_back, axis=-1)
    d_gate = down_back * up_lin * gate_sig * (1.0 + gate_lin * (1.0 - gate_sig))
    d_up = down_back * gate_act
    scale_col = slot_w.astype(jnp.float32)[..., None]
    return (
        d_gate.astype(jnp.bfloat16),
        d_up.astype(jnp.bfloat16),
        slot_score,
        (scale_col * d_gate).astype(jnp.bfloat16),
        (scale_col * d_up).astype(jnp.bfloat16),
        (scale_col * hidden).astype(jnp.bfloat16),
    )


def weight_grads(rows_x, rows_z, gate_wt, up_wt, hidden_wt):
    grad_gate = jnp.einsum(
        "esd,esh->edh", rows_x, gate_wt, preferred_element_type=jnp.float32
    ).astype(jnp.bfloat16)
    grad_up = jnp.einsum("esd,esh->edh", rows_x, up_wt, preferred_element_type=jnp.float32).astype(
        jnp.bfloat16
    )
    grad_down = jnp.einsum(
        "esh,esd->ehd", hidden_wt, rows_z, preferred_element_type=jnp.float32
    ).astype(jnp.bfloat16)
    return (grad_gate, grad_up, grad_down)


def slot_total(slot_score):
    return lax.psum(slot_score, "expert")


def finish_tokens(
    returned_rows,
    score_rows,
    hits,
    picked,
    pick_sum,
    weights,
    normed_part,
    centered_scaled_slice,
    amp_part,
    inverse_deviation,
    output_gradient_slice,
    router_w,
    entire_width,
):
    highest = lax.Precision.HIGHEST
    tok_rows = weights.shape[0]
    paired = returned_rows.reshape(tok_rows, 2, -1)
    combined = weights[:, 0:1] * paired[:, 0] + weights[:, 1:2] * paired[:, 1]
    score_pair = score_rows.reshape(tok_rows, 2)
    mean_score = jnp.sum(weights * score_pair, axis=1, keepdims=True)
    d_pick = (score_pair - mean_score) / pick_sum * picked * (1.0 - picked)
    dlogit = jnp.sum(jnp.where(hits, d_pick[:, :, None], 0.0), axis=1)
    dnormed = combined + jnp.einsum("te,de->td", dlogit, router_w, precision=highest)
    grad_router = lax.psum(jnp.einsum("td,te->de", normed_part, dlogit, precision=highest), "dp")
    normalized_gradient = dnormed * amp_part
    first_sum, second_sum = lax.psum(
        (
            jnp.sum(normalized_gradient, axis=1, keepdims=True),
            jnp.sum(normalized_gradient * centered_scaled_slice, axis=1, keepdims=True),
        ),
        "expert",
    )
    latent_gradient = (
        inverse_deviation
        * (
            normalized_gradient
            - first_sum / entire_width
            - centered_scaled_slice * (second_sum / entire_width)
        )
        + output_gradient_slice
    )
    return (latent_gradient.astype(jnp.bfloat16), grad_router)


def per_device(
    latents, cotangent, routes, router_w, mod_shift, mod_scale, mod_gate, gate_w, up_w, down_w
):
    highest = lax.Precision.HIGHEST
    tok_rows = latents.shape[0]
    slice_width = latents.shape[1]
    experts = router_w.shape[1]
    local = gate_w.shape[0]
    groups = lax.axis_size("dp")
    entire_width = slice_width * lax.axis_size("expert")
    capacity = 3 * tok_rows // experts
    slot_count = experts * capacity
    sample_index = lax.axis_index("dp") * tok_rows // SEQ
    column_offset = lax.axis_index("expert") * slice_width
    targets = slot_targets(routes, experts, capacity)
    output_gradient_slice = cotangent.astype(jnp.float32)
    whole_x, whole_dy, entire_shift, whole_scale, whole_gate = (
        lax.all_gather(latents, "expert", axis=1, tiled=True),
        lax.all_gather(cotangent, "expert", axis=1, tiled=True),
        lax.all_gather(mod_shift, "expert", axis=1, tiled=True),
        lax.all_gather(mod_scale, "expert", axis=1, tiled=True),
        lax.all_gather(mod_gate, "expert", axis=1, tiled=True),
    )
    router_full = lax.all_gather(
        router_w.astype(jnp.bfloat16), "expert", axis=0, tiled=True
    ).astype(router_w.dtype)
    latent_rows_f32 = whole_x.astype(jnp.float32)
    row_average = jnp.mean(latent_rows_f32, axis=1, keepdims=True)
    row_msq = jnp.mean(latent_rows_f32 * latent_rows_f32, axis=1, keepdims=True)
    inverse_deviation = lax.rsqrt(row_msq - row_average * row_average + norm_eps)
    centered_scaled = (latent_rows_f32 - row_average) * inverse_deviation
    modulation_amplitude = 1.0 + selected_row(whole_scale, sample_index)
    normed_rows = centered_scaled * modulation_amplitude + selected_row(entire_shift, sample_index)
    normed_b = normed_rows.astype(jnp.bfloat16)
    logits = jnp.dot(normed_rows, router_full, precision=highest)
    hits, picked, pick_sum, weights = route_weights(logits, routes, experts)
    scaled_dy = (selected_row(whole_gate, sample_index) * whole_dy.astype(jnp.float32)).astype(
        jnp.bfloat16
    )
    send_x, send_z, send_w = fill_slots(
        normed_b, scaled_dy, weights.astype(jnp.bfloat16), targets, slot_count
    )
    got_x, got_z, got_w = (
        lax.all_to_all(
            send_x.reshape(experts, capacity, entire_width),
            "dp",
            split_axis=0,
            concat_axis=0,
            tiled=True,
        ),
        lax.all_to_all(
            send_z.reshape(experts, capacity, entire_width),
            "dp",
            split_axis=0,
            concat_axis=0,
            tiled=True,
        ),
        lax.all_to_all(
            send_w.reshape(experts, capacity), "dp", split_axis=0, concat_axis=0, tiled=True
        ),
    )
    rows_x = owner_view(got_x, groups, local)
    rows_z = owner_view(got_z, groups, local)
    slot_w = owner_view(got_w, groups, local)
    gate_lin = jnp.einsum("esd,edh->esh", rows_x, gate_w, preferred_element_type=jnp.float32)
    up_lin = jnp.einsum("esd,edh->esh", rows_x, up_w, preferred_element_type=jnp.float32)
    down_back = jnp.einsum("esd,ehd->esh", rows_z, down_w, preferred_element_type=jnp.float32)
    d_gate_b, d_up_b, slot_score, gate_wt, up_wt, hidden_wt = expert_grads(
        gate_lin, up_lin, down_back, slot_w
    )
    grad_gate, grad_up, grad_down = weight_grads(rows_x, rows_z, gate_wt, up_wt, hidden_wt)
    part_rows = (
        jnp.einsum("esh,edh->esd", d_gate_b, gate_w, preferred_element_type=jnp.float32)
        + jnp.einsum("esh,edh->esd", d_up_b, up_w, preferred_element_type=jnp.float32)
    ).astype(jnp.bfloat16)
    score_sum = slot_total(slot_score)
    back_rows = lax.all_to_all(
        sender_view(part_rows, groups), "dp", split_axis=0, concat_axis=0, tiled=True
    )
    back_scores = lax.all_to_all(
        sender_view(score_sum, groups), "dp", split_axis=0, concat_axis=0, tiled=True
    )
    summed = lax.psum_scatter(
        back_rows.reshape(slot_count, entire_width).astype(jnp.float32).astype(jnp.bfloat16),
        "expert",
        scatter_dimension=1,
        tiled=True,
    ).astype(jnp.float32)
    returned_rows = summed[targets]
    score_rows = back_scores.reshape(-1)[targets]
    centered_scaled_slice = lax.dynamic_slice_in_dim(centered_scaled, column_offset, slice_width, 1)
    amp_part = lax.dynamic_slice_in_dim(modulation_amplitude, column_offset, slice_width, 1)
    normed_part = lax.dynamic_slice_in_dim(normed_rows, column_offset, slice_width, 1)
    latent_gradient, grad_router = finish_tokens(
        returned_rows,
        score_rows,
        hits,
        picked,
        pick_sum,
        weights,
        normed_part,
        centered_scaled_slice,
        amp_part,
        inverse_deviation,
        output_gradient_slice,
        router_w,
        entire_width,
    )
    return (latent_gradient, grad_gate, grad_up, grad_down, grad_router)


def solution(mesh):
    placed = (
        P("dp", "expert"),
        P("dp", "expert"),
        P("dp", None),
        P("expert", None),
        P(None, "expert"),
        P(None, "expert"),
        P(None, "expert"),
        P("dp", None, "expert"),
        P("dp", None, "expert"),
        P("dp", "expert", None),
    )
    return jax.shard_map(
        per_device,
        mesh=mesh,
        in_specs=placed,
        out_specs=(
            P("dp", "expert"),
            P("dp", None, "expert"),
            P("dp", None, "expert"),
            P("dp", "expert", None),
            P("expert", None),
        ),
        check_vma=False,
    )
```

profile of v0, /device:TPU:0, one launch (start us, length us, event | category | flops | bytes accessed | tf_op | source)
XLA Modules:
  0.0 442.6 jit_solution(14642404818928266631)
XLA Ops:
  7.2 0.7 all-gather.3.cloned.1.call-update
  7.9 0.7 broadcast_multiply_fusion
  8.6 0.8 copy.35
  9.4 0.1 eq.45
  9.6 0.1 eq.41
  9.7 2.1 all_gather.20
  11.8 0.1 copy.34
  12.0 0.1 mul.200
  12.1 1.2 reduce-window.6
  13.3 0.2 slice_reduce_fusion
  13.5 1.9 all_gather.19
  15.6 5.7 %all-gather.3.cloned.1.call-done = bf16[256,2048]{1,0:T(8,128)(2,1)} async-done(((bf16[256,1024]{1,0:T(8,128)(2,1)}), bf16[256,2048]{1,0:T(8,128)(2,1)}) %all-gather.3.cloned.1.call-update) | async-done | bytes 1048592 | tf_op jit(solution)/shard_map/all_gather | solution.py:158
  21.3 1.7 convert_reduce_fusion
  23.0 3.8 multiply_add_fusion
  26.9 2.6 broadcast_in_dim.35
  29.4 4.1 reshape.288
  33.5 6.7 %scatter_custom_fusion.1 = bf16[768,2048]{1,0:T(8,128)(2,1)} fusion(s32[512]{0:T(512)S(1)} %bitcast.91, bf16[512,2048]{1,0:T(8,128)(2,1)} %reshape.288, bf16[]{:T(256)} %constant.21.clone.1), kind=kCustom, calls=%fused_computation.35 | custom fusion | bytes 3146240 | tf_op jit(solution)/shard_map/scatter | solution.py:50
  40.3 7.0 %all-to-all-start.1 = ((bf16[16,48,2048]{2,1,0:T(8,128)(2,1)}), bf16[16,48,2048]{2,1,0:T(8,128)(2,1)}, u32[]{:S(2)}, u32[]{:S(2)}) async-start(bf16[16,48,2048]{2,1,0:T(8,128)(2,1)} %bitcast.82), calls=%async_computation.1 | async-start | bytes 6291456 | tf_op jit(solution)/shard_map/all_to_all | solution.py:184
  47.3 0.7 all-gather.5.cloned.1.call-update
  48.0 2.1 all_gather.22
  50.2 9.8 %all-gather.5.cloned.1.call-done = bf16[256,2048]{1,0:T(8,128)(2,1)} async-done(((bf16[256,1024]{1,0:T(8,128)(2,1)}), bf16[256,2048]{1,0:T(8,128)(2,1)}) %all-gather.5.cloned.1.call-update) | async-done | bytes 1048592 | tf_op jit(solution)/shard_map/all_gather | solution.py:159
  59.9 1.5 multiply_convert_fusion
  61.4 2.6 broadcast_in_dim.34
  64.0 4.1 reshape.280
  68.1 6.7 %scatter_custom_fusion = bf16[768,2048]{1,0:T(8,128)(2,1)} fusion(s32[512]{0:T(512)S(1)} %bitcast.92, bf16[512,2048]{1,0:T(8,128)(2,1)} %reshape.280, bf16[]{:T(256)} %constant.21.clone.1), kind=kCustom, calls=%fused_computation.37 | custom fusion | bytes 3146240 | tf_op jit(solution)/shard_map/scatter | solution.py:55
  74.9 33.7 %all-to-all-done.1 = bf16[16,48,2048]{2,1,0:T(8,128)(2,1)} async-done(((bf16[16,48,2048]{2,1,0:T(8,128)(2,1)}), bf16[16,48,2048]{2,1,0:T(8,128)(2,1)}, u32[]{:S(2)}, u32[]{:S(2)}) %all-to-all-start.1) | async-done | bytes 3145760 | tf_op jit(solution)/shard_map/all_to_all | solution.py:184
  108.6 16.2 %all-to-all-start = ((bf16[16,48,2048]{2,1,0:T(8,128)(2,1)}), bf16[16,48,2048]{2,1,0:T(8,128)(2,1)}, u32[]{:S(2)}, u32[]{:S(2)}) async-start(bf16[16,48,2048]{2,1,0:T(8,128)(2,1)} %bitcast.83), calls=%async_computation | async-start | bytes 6291456 | tf_op jit(solution)/shard_map/all_to_all | solution.py:191
  124.8 0.6 reduce-scatter.2.cloned.1.call-start
  125.4 5.0 %fusion.7 = f32[768,512]{0,1:T(8,128)} fusion(bf16[768,2048]{1,0:T(8,128)(2,1)} %bitcast.11, bf16[1,2048,512]{2,1,0:T(8,128)(2,1)S(1)} %copy-done), kind=kOutput, calls=%fused_computation.19 | convolution fusion | flops 1610612736 | bytes 6815744 | tf_op jit(solution)/shard_map/esd,edh->esh/dot_general | solution.py:205
  130.4 4.9 %fusion.10 = f32[768,512]{0,1:T(8,128)} fusion(bf16[768,2048]{1,0:T(8,128)(2,1)} %bitcast.11, bf16[1,2048,512]{2,1,0:T(8,128)(2,1)S(1)} %copy-done.8), kind=kOutput, calls=%fused_computation.22 | convolution fusion | flops 1610612736 | bytes 6815744 | tf_op jit(solution)/shard_map/esd,edh->esh/dot_general | solution.py:206
  135.3 50.2 %all-to-all-done = bf16[16,48,2048]{2,1,0:T(8,128)(2,1)} async-done(((bf16[16,48,2048]{2,1,0:T(8,128)(2,1)}), bf16[16,48,2048]{2,1,0:T(8,128)(2,1)}, u32[]{:S(2)}, u32[]{:S(2)}) %all-to-all-start) | async-done | bytes 3145760 | tf_op jit(solution)/shard_map/all_to_all | solution.py:191
  185.5 5.5 %multiply_reduce_fusion = (f32[768]{0:T(1024)S(1)}, f32[768,512]{0,1:T(8,128)S(1)}) fusion(f32[768,512]{0,1:T(8,128)} %fusion.10, f32[768,512]{0,1:T(8,128)} %fusion.7, bf16[768,2048]{1,0:T(8,128)(2,1)} %bitcast.8, bf16[1,512,2048]{2,1,0:T(8,128)(2,1)} %param.19), kind=kOutput, calls=%fused_computation.31 | convolution fusion | flops 1613364480 | bytes 9964544 | tf_op jit(solution)/shard_map/esd,ehd->esh/dot_general | solution.py:207
  191.1 2.3 fusion.5
  193.4 1.9 add_convert_fusion
  195.4 84.8 %all_to_all.34 = bf16[16,48,2048]{2,1,0:T(8,128)(2,1)} all-to-all(bf16[16,48,2048]{2,1,0:T(8,128)(2,1)S(1)} %bitcast.84), channel_id=1, replica_groups=mesh['dp'=16,'expert'=2] {'dp'}, dimensions={0} | all-to-all | bytes 6291456 | tf_op jit(solution)/shard_map/all_to_all | solution.py:217
  280.2 0.8 copy-done.5
  281.0 2.0 all_gather.21
  283.0 1.5 fusion.22
  284.6 0.1 copy.42
  284.7 0.1 reshape.296
  284.9 3.8 scatter_custom_fusion.2
  288.6 0.7 all_to_all.28
  289.3 4.0 all-to-all-start.4
  293.3 7.2 %all-to-all-done.4 = bf16[16,1,48]{2,1,0:T(2,128)(2,1)S(1)} async-done(((bf16[16,1,48]{2,1,0:T(2,128)(2,1)}), bf16[16,1,48]{2,1,0:T(2,128)(2,1)S(1)}, u32[]{:S(2)}, u32[]{:S(2)}) %all-to-all-start.4) | async-done | bytes 1568 | tf_op jit(solution)/shard_map/all_to_all | solution.py:198
  300.8 3.1 psum.28
  303.8 3.5 all-to-all-start.3
  307.3 0.3 all-reduce.3.cloned.1.call-start
  307.6 6.2 %fusion.1 = bf16[1,2048,512]{2,1,0:T(8,128)(2,1)} fusion(bf16[768,2048]{1,0:T(8,128)(2,1)} %bitcast.11, f32[768]{0:T(1024)S(1)} %reshape.259, f32[768,512]{0,1:T(8,128)} %copy-done.12, f32[768,512]{0,1:T(8,128)} %fusion.7), kind=kOutput, calls=%fused_computation.13 | convolution fusion | flops 1614413824 | bytes 8391680 | tf_op jit(solution)/shard_map/esd,esh->edh/dot_general | solution.py:83
  313.9 5.2 %fusion = bf16[1,2048,512]{2,1,0:T(8,128)(2,1)} fusion(bf16[768,2048]{1,0:T(8,128)(2,1)} %bitcast.11, f32[768]{0:T(1024)S(1)} %reshape.259, f32[768,512]{0,1:T(8,128)S(1)} %copy-done.11, f32[768,512]{0,1:T(8,128)S(1)} %copy-done.13, f32[768,512]{0,1:T(8,128)S(1)} %copy-done.15), kind=kOutput, calls=%fused_computation.12 | convolution fusion | flops 1615986688 | bytes 9964544 | tf_op jit(solution)/shard_map/esd,esh->edh/dot_general | solution.py:80
  319.1 5.1 %fusion.2 = bf16[1,512,2048]{2,1,0:T(8,128)(2,1)} fusion(bf16[768,2048]{1,0:T(8,128)(2,1)} %bitcast.8, f32[768]{0:T(1024)S(1)} %reshape.259, f32[768,512]{0,1:T(8,128)S(1)} %copy-done.15, f32[768,512]{0,1:T(8,128)S(1)} %copy-done.11), kind=kOutput, calls=%fused_computation.14 | convolution fusion | flops 1614413824 | bytes 8391680 | tf_op jit(solution)/shard_map/esh,esd->ehd/dot_general | solution.py:86
  324.2 0.5 broadcast.185
  324.7 0.8 reduce.12
  325.6 2.3 gather_fusion.1
  327.9 0.1 reshape.255
  328.1 1.3 fusion.26
  329.5 1.8 convert_element_type.108
  331.3 2.7 gather_fusion
  334.0 2.5 reshape.253
  336.5 1.6 fusion.49
  338.2 1.5 fusion.47
  339.7 2.5 all-reduce
  342.2 2.5 add_convert_fusion.1
  344.7 89.7 %all-reduce.3.cloned.1.call-done = f32[1024,16]{0,1:T(8,128)} async-done(((f32[1024,16]{0,1:T(8,128)}), f32[1024,16]{0,1:T(8,128)}) %all-reduce.3.cloned.1.call-update) | async-done | bytes 65552 | tf_op jit(solution)/shard_map/psum | solution.py:120
  434.4 1.5 copy.61
  (61 shorter events, 0.8 us)
Async XLA Ops:
  7.2 118.2 %copy-start = (bf16[1,2048,512]{2,1,0:T(8,128)(2,1)S(1)}, bf16[1,2048,512]{2,1,0:T(8,128)(2,1)}, u32[]{:S(2)}) copy-start(bf16[1,2048,512]{2,1,0:T(8,128)(2,1)} %param.17) | copy-start | bytes 6291460
  7.2 14.1 %all-gather.3.cloned.1.call-start = ((), (), s32[]{:S(2)}) async-start(), calls=%async_computation.6 | async-start | bytes 1572864 | tf_op jit(solution)/shard_map/all_gather | solution.py:158
  40.3 7.7 %copy-start.7 = (bf16[1,1024]{1,0:T(2,128)(2,1)S(1)}, bf16[1,1024]{1,0:T(2,128)(2,1)}, u32[]{:S(2)}) copy-start(bf16[1,1024]{1,0:T(2,128)(2,1)} %param.16) | copy-start | bytes 6148
  40.3 68.3 %all-to-all-start.1 = ((bf16[16,48,2048]{2,1,0:T(8,128)(2,1)}), bf16[16,48,2048]{2,1,0:T(8,128)(2,1)}, u32[]{:S(2)}, u32[]{:S(2)}) async-start(bf16[16,48,2048]{2,1,0:T(8,128)(2,1)} %bitcast.82), calls=%async_computation.1 | async-start | bytes 6291456 | tf_op jit(solution)/shard_map/all_to_all | solution.py:184
  47.3 12.7 %all-gather.5.cloned.1.call-start = ((), (), s32[]{:S(2)}) async-start(), calls=%async_computation.7 | async-start | bytes 1572864 | tf_op jit(solution)/shard_map/all_gather | solution.py:159
  108.6 76.9 %all-to-all-start = ((bf16[16,48,2048]{2,1,0:T(8,128)(2,1)}), bf16[16,48,2048]{2,1,0:T(8,128)(2,1)}, u32[]{:S(2)}, u32[]{:S(2)}) async-start(bf16[16,48,2048]{2,1,0:T(8,128)(2,1)} %bitcast.83), calls=%async_computation | async-start | bytes 6291456 | tf_op jit(solution)/shard_map/all_to_all | solution.py:191
  124.8 204.7 %reduce-scatter.2.cloned.1.call-start = ((), (), s32[]{:S(2)}) async-start(), calls=%async_computation.8 | async-start | bytes 4718592 | tf_op jit(solution)/shard_map/reduce_scatter | solution.py:223
  125.4 5.0 %copy-start.8 = (bf16[1,2048,512]{2,1,0:T(8,128)(2,1)S(1)}, bf16[1,2048,512]{2,1,0:T(8,128)(2,1)}, u32[]{:S(2)}) copy-start(bf16[1,2048,512]{2,1,0:T(8,128)(2,1)} %param.18) | copy-start | bytes 6291460
  185.5 5.5 %copy-start.10 = (f32[768,512]{0,1:T(8,128)S(1)}, f32[768,512]{0,1:T(8,128)}, u32[]{:S(2)}) copy-start(f32[768,512]{0,1:T(8,128)} %fusion.7) | copy-start | bytes 4718596
  185.5 5.6 %copy-start.14 = (f32[768,512]{0,1:T(8,128)S(1)}, f32[768,512]{0,1:T(8,128)}, u32[]{:S(2)}) copy-start(f32[768,512]{0,1:T(8,128)} %fusion.10) | copy-start | bytes 4718596
  191.1 2.4 copy-start.12
  191.1 2.3 copy-start.9
  280.2 0.8 copy-start.5
  280.2 2.9 copy-start.4
  280.2 4.3 copy-start.6
  289.3 11.2 %all-to-all-start.4 = ((bf16[16,1,48]{2,1,0:T(2,128)(2,1)}), bf16[16,1,48]{2,1,0:T(2,128)(2,1)S(1)}, u32[]{:S(2)}, u32[]{:S(2)}) async-start(bf16[16,1,48]{2,1,0:T(2,128)(2,1)} %all_to_all.28), calls=%async_computation.5 | async-start | bytes 16384 | tf_op jit(solution)/shard_map/all_to_all | solution.py:198
  303.8 20.3 %all-to-all-start.3 = ((f32[16,1,48]{2,1,0:T(1,128)}), f32[16,1,48]{2,1,0:T(1,128)S(1)}, u32[]{:S(2)}, u32[]{:S(2)}) async-start(f32[16,1,48]{2,1,0:T(1,128)} %psum.28), calls=%async_computation.4 | async-start | bytes 16384 | tf_op jit(solution)/shard_map/all_to_all | solution.py:220
  307.3 6.5 %copy-start.11 = (f32[768,512]{0,1:T(8,128)S(1)}, f32[768,512]{0,1:T(8,128)}, u32[]{:S(2)}) copy-start(f32[768,512]{0,1:T(8,128)} %fusion.7) | copy-start | bytes 4718596
  307.3 127.0 %all-reduce.3.cloned.1.call-start = ((), (), s32[]{:S(2)}) async-start(), calls=%async_computation.9 | async-start | bytes 131072 | tf_op jit(solution)/shard_map/psum | solution.py:120
  307.6 6.3 %copy-start.13 = (f32[768,512]{0,1:T(8,128)S(1)}, f32[768,512]{0,1:T(8,128)}, u32[]{:S(2)}) copy-start(f32[768,512]{0,1:T(8,128)} %copy-done.12) | copy-start | bytes 4718596
  307.6 6.3 %copy-start.15 = (f32[768,512]{0,1:T(8,128)S(1)}, f32[768,512]{0,1:T(8,128)}, u32[]{:S(2)}) copy-start(f32[768,512]{0,1:T(8,128)} %fusion.10) | copy-start | bytes 4718596
  324.2 4.0 copy-start.3
  336.5 1.6 copy-start.2
  338.2 97.7 %copy-start.1 = (bf16[1,2048,512]{2,1,0:T(8,128)(2,1)S(1)}, bf16[1,2048,512]{2,1,0:T(8,128)(2,1)}, u32[]{:S(2)}) copy-start(bf16[1,2048,512]{2,1,0:T(8,128)(2,1)} %param.17) | copy-start | bytes 6291460
Sparse Core Ops, SparseCore 0:
  9.5 11.7 all-gather.2
  49.6 10.2 all-gather.4
  280.3 9.3 reduce-scatter.1
  329.6 104.7 all-reduce.2
where the time goes:
time: 450 us; the launch traced here: 443 us
  waiting for transfers between devices  198 us (44%)
  blocking collectives  98.5 us (22%)
  local copies, waits for them, and re-layouts  45.6 us (10%)
  matrix products  40.5 us (9%)
  starting transfers between devices  31.5 us (7%)
  between operations  14.4 us (3%)
  other arithmetic  14.2 us (3%)
    psum x1, waiting for transfers between devices, finish_tokens(): lax.psum(jnp.einsum('td,te->de', normed_part, dlogit, precision=highest),...  89.7 us
    all_to_all x1, blocking collectives, per_device(): lax.all_to_all(sender_view(part_rows, groups), 'dp', split_axis=0, concat...  84.8 us
    all_to_all x1, waiting for transfers between devices, per_device(): lax.all_to_all(send_z.reshape(experts, capacity, entire_width), 'dp', spl...  50.2 us
    all_to_all x1, waiting for transfers between devices, per_device(): lax.all_to_all(send_x.reshape(experts, capacity, entire_width), 'dp', spl...  33.7 us
    all_to_all x1, starting transfers between devices, per_device(): lax.all_to_all(send_z.reshape(experts, capacity, entire_width), 'dp', spl...  16.2 us
    all_gather x1, waiting for transfers between devices, per_device(): lax.all_gather(cotangent, 'expert', axis=1, tiled=True)  9.78 us
  transfers between devices with their start and end apart: 8, of which 6 were waited for; matrix products, arithmetic and copies ran while one was open for 15% of the time, Pallas kernels for 0%

commit v1 on v0

--- a/solution.py
+++ b/solution.py
@@ -117,7 +117,8 @@
     d_pick = (score_pair - mean_score) / pick_sum * picked * (1.0 - picked)
     dlogit = jnp.sum(jnp.where(hits, d_pick[:, :, None], 0.0), axis=1)
     dnormed = combined + jnp.einsum("te,de->td", dlogit, router_w, precision=highest)
-    grad_router = lax.psum(jnp.einsum("td,te->de", normed_part, dlogit, precision=highest), "dp")
+    pieces_all_turn = lambda z_in: jnp.sum(lax.all_gather(z_in, "dp"), axis=0)
+    grad_router = pieces_all_turn(jnp.einsum("td,te->de", normed_part, dlogit, precision=highest))
     normalized_gradient = dnormed * amp_part
     first_sum, second_sum = lax.psum(
         (

time: 450 us -> 368 us (0.82)
  blocking collectives: 98.5 us -> 13.7 us
  waiting for transfers between devices: 198 us -> 161 us
  starting transfers between devices: 31.5 us -> 60.5 us
  matrix products: 40.5 us -> 49.1 us
    psum x1 -> x0, waiting for transfers between devices: 89.7 us -> none  [finish_tokens(): lax.psum(jnp.einsum('td,te->de', normed_part, dlogit, precision=highest),...]
    all_to_all x1 -> x0, blocking collectives: 84.8 us -> none  [per_device(): lax.all_to_all(sender_view(part_rows, groups), 'dp', split_axis=0, concat...]
    all_to_all x0 -> x1, waiting for transfers between devices: none -> 52.8 us  [per_device(): lax.all_to_all(sender_view(part_rows, groups), 'dp', split_axis=0, concat...]
    all_to_all x1, starting transfers between devices: 4.01 us -> 16 us  [per_device(): lax.all_to_all(send_w.reshape(experts, capacity), 'dp', split_axis=0, con...]
    all_to_all x1, starting transfers between devices: 3.47 us -> 14.1 us  [per_device(): lax.all_to_all(sender_view(score_sum, groups), 'dp', split_axis=0, concat...]
    all_to_all x0 -> x1, starting transfers between devices: none -> 7.03 us  [per_device(): lax.all_to_all(sender_view(part_rows, groups), 'dp', split_axis=0, concat...]
  transfers between devices with their start and end apart: 8 -> 9, of which waited for: 6 -> 6; matrix products, arithmetic and copies ran while one was open for 15% -> 19% of each run, Pallas kernels for 0% -> 0%
where the time goes in v1:
time: 368 us; the launch traced here: 361 us
  waiting for transfers between devices  161 us (44%)
  starting transfers between devices  60.5 us (16%)
  matrix products  49.1 us (13%)
  local copies, waits for them, and re-layouts  46.9 us (13%)
  other arithmetic  14.8 us (4%)
  between operations  14.4 us (4%)
  blocking collectives  13.7 us (4%)
    all_to_all x1, waiting for transfers between devices, per_device(): lax.all_to_all(sender_view(part_rows, groups), 'dp', split_axis=0, concat...  52.8 us
    all_to_all x1, waiting for transfers between devices, per_device(): lax.all_to_all(send_z.reshape(experts, capacity, entire_width), 'dp', spl...  50.8 us
    all_to_all x1, waiting for transfers between devices, per_device(): lax.all_to_all(send_x.reshape(experts, capacity, entire_width), 'dp', spl...  33.7 us
    all_to_all x1, starting transfers between devices, per_device(): lax.all_to_all(send_z.reshape(experts, capacity, entire_width), 'dp', spl...  16.2 us
    all_to_all x1, starting transfers between devices, per_device(): lax.all_to_all(send_w.reshape(experts, capacity), 'dp', split_axis=0, con...  16 us
    all_to_all x1, starting transfers between devices, per_device(): lax.all_to_all(sender_view(score_sum, groups), 'dp', split_axis=0, concat...  14.1 us
    all_gather x1, waiting for transfers between devices, per_device(): lax.all_gather(cotangent, 'expert', axis=1, tiled=True)  9.61 us
  transfers between devices with their start and end apart: 9, of which 6 were waited for; matrix products, arithmetic and copies ran while one was open for 19% of the time, Pallas kernels for 0%

profile of v1, /device:TPU:0, one launch (start us, length us, event | category | flops | bytes accessed | tf_op | source)
XLA Modules:
  0.0 360.8 jit_solution(1580853472096654611)
XLA Ops:
  7.2 0.7 all-gather.5.cloned.1.call-update
  7.9 0.7 broadcast_multiply_fusion
  8.6 0.8 copy.35
  9.4 0.1 eq.45
  9.6 0.1 eq.41
  9.7 2.1 all_gather.26
  11.8 0.1 copy.34
  12.0 0.1 mul.200
  12.1 1.2 reduce-window.6
  13.3 0.2 slice_reduce_fusion
  13.5 1.9 all_gather.25
  15.5 0.1 fusion.37
  15.6 5.7 %all-gather.5.cloned.1.call-done = bf16[256,2048]{1,0:T(8,128)(2,1)} async-done(((bf16[256,1024]{1,0:T(8,128)(2,1)}), bf16[256,2048]{1,0:T(8,128)(2,1)}) %all-gather.5.cloned.1.call-update) | async-done | bytes 1048592 | tf_op jit(solution)/shard_map/all_gather | solution.py:159
  21.3 1.7 convert_reduce_fusion
  23.0 3.8 %multiply_add_fusion = (f32[256,2048]{1,0:T(8,128)}, bf16[256,2048]{1,0:T(8,128)(2,1)S(1)}, f32[256,2048]{1,0:T(8,128)}) fusion(f32[2048]{0:T(1024)S(1)} %bitcast.93, f32[2048]{0:T(1024)S(1)} %bitcast.91, f32[256]{0:T(256)S(1)} %get-tuple-element.23, f32[256]{0:T(256)S(1)} %get-tuple-element.22, bf16[256,2048]{1,0:T(8,128)(2,1)} %all-gather.5.cloned.1.call-done), kind=kLoop, calls=%fused_computation.27 | loop fusion | flops 3145728 | bytes 6309888 | tf_op jit(solution)/shard_map/add | solution.py:174
  26.8 2.6 broadcast_in_dim.35
  29.4 4.1 %reshape.288 = bf16[512,2048]{1,0:T(8,128)(2,1)} reshape(bf16[256,2,2048]{2,1,0:T(2,128)(2,1)} %broadcast_in_dim.35) | data formatting | bytes 4194304 | tf_op jit(solution)/shard_map/reshape | solution.py:50
  33.5 6.7 %scatter_custom_fusion.1 = bf16[768,2048]{1,0:T(8,128)(2,1)} fusion(s32[512]{0:T(512)S(1)} %bitcast.97, bf16[512,2048]{1,0:T(8,128)(2,1)} %reshape.288, bf16[]{:T(256)} %constant.21.clone.1), kind=kCustom, calls=%fused_computation.35 | custom fusion | bytes 3146240 | tf_op jit(solution)/shard_map/scatter | solution.py:50
  40.2 7.0 %all-to-all-start.1 = ((bf16[16,48,2048]{2,1,0:T(8,128)(2,1)}), bf16[16,48,2048]{2,1,0:T(8,128)(2,1)}, u32[]{:S(2)}, u32[]{:S(2)}) async-start(bf16[16,48,2048]{2,1,0:T(8,128)(2,1)} %bitcast.87), calls=%async_computation.1 | async-start | bytes 6291456 | tf_op jit(solution)/shard_map/all_to_all | solution.py:185
  47.3 0.7 all-gather.7.cloned.1.call-update
  48.0 2.3 all_gather.28
  50.3 9.6 %all-gather.7.cloned.1.call-done = bf16[256,2048]{1,0:T(8,128)(2,1)} async-done(((bf16[256,1024]{1,0:T(8,128)(2,1)}), bf16[256,2048]{1,0:T(8,128)(2,1)}) %all-gather.7.cloned.1.call-update) | async-done | bytes 1048592 | tf_op jit(solution)/shard_map/all_gather | solution.py:160
  59.9 1.5 multiply_convert_fusion
  61.4 2.6 broadcast_in_dim.34
  64.0 4.1 %reshape.280 = bf16[512,2048]{1,0:T(8,128)(2,1)} reshape(bf16[256,2,2048]{2,1,0:T(2,128)(2,1)} %broadcast_in_dim.34) | data formatting | bytes 4194304 | tf_op jit(solution)/shard_map/reshape | solution.py:55
  68.1 6.7 %scatter_custom_fusion = bf16[768,2048]{1,0:T(8,128)(2,1)} fusion(s32[512]{0:T(512)S(1)} %bitcast.98, bf16[512,2048]{1,0:T(8,128)(2,1)} %reshape.280, bf16[]{:T(256)} %constant.21.clone.1), kind=kCustom, calls=%fused_computation.37 | custom fusion | bytes 3146240 | tf_op jit(solution)/shard_map/scatter | solution.py:55
  74.8 33.7 %all-to-all-done.1 = bf16[16,48,2048]{2,1,0:T(8,128)(2,1)} async-done(((bf16[16,48,2048]{2,1,0:T(8,128)(2,1)}), bf16[16,48,2048]{2,1,0:T(8,128)(2,1)}, u32[]{:S(2)}, u32[]{:S(2)}) %all-to-all-start.1) | async-done | bytes 3145760 | tf_op jit(solution)/shard_map/all_to_all | solution.py:185
  108.5 16.2 %all-to-all-start = ((bf16[16,48,2048]{2,1,0:T(8,128)(2,1)}), bf16[16,48,2048]{2,1,0:T(8,128)(2,1)}, u32[]{:S(2)}, u32[]{:S(2)}) async-start(bf16[16,48,2048]{2,1,0:T(8,128)(2,1)} %bitcast.88), calls=%async_computation | async-start | bytes 6291456 | tf_op jit(solution)/shard_map/all_to_all | solution.py:192
  124.8 5.0 %fusion.7 = f32[768,512]{0,1:T(8,128)} fusion(bf16[768,2048]{1,0:T(8,128)(2,1)} %bitcast.11, bf16[1,2048,512]{2,1,0:T(8,128)(2,1)S(1)} %copy-done), kind=kOutput, calls=%fused_computation.19 | convolution fusion | flops 1610612736 | bytes 6815744 | tf_op jit(solution)/shard_map/esd,edh->esh/dot_general | solution.py:206
  129.8 4.9 %fusion.10 = f32[768,512]{0,1:T(8,128)} fusion(bf16[768,2048]{1,0:T(8,128)(2,1)} %bitcast.11, bf16[1,2048,512]{2,1,0:T(8,128)(2,1)S(1)} %copy-done.7), kind=kOutput, calls=%fused_computation.22 | convolution fusion | flops 1610612736 | bytes 6815744 | tf_op jit(solution)/shard_map/esd,edh->esh/dot_general | solution.py:207
  134.7 50.8 %all-to-all-done = bf16[16,48,2048]{2,1,0:T(8,128)(2,1)} async-done(((bf16[16,48,2048]{2,1,0:T(8,128)(2,1)}), bf16[16,48,2048]{2,1,0:T(8,128)(2,1)}, u32[]{:S(2)}, u32[]{:S(2)}) %all-to-all-start) | async-done | bytes 3145760 | tf_op jit(solution)/shard_map/all_to_all | solution.py:192
  185.5 6.5 %multiply_reduce_fusion = (f32[768]{0:T(1024)S(1)}, f32[768,512]{0,1:T(8,128)}) fusion(f32[768,512]{0,1:T(8,128)} %fusion.10, f32[768,512]{0,1:T(8,128)} %fusion.7, bf16[768,2048]{1,0:T(8,128)(2,1)} %bitcast.8, bf16[1,512,2048]{2,1,0:T(8,128)(2,1)} %param.19), kind=kOutput, calls=%fused_computation.31 | convolution fusion | flops 1613364480 | bytes 9964544 | tf_op jit(solution)/shard_map/esd,ehd->esh/dot_general | solution.py:208
  192.0 3.1 psum.21
  195.1 14.1 %all-to-all-start.3 = ((f32[16,1,48]{2,1,0:T(1,128)}), f32[16,1,48]{2,1,0:T(1,128)S(1)}, u32[]{:S(2)}, u32[]{:S(2)}) async-start(f32[16,1,48]{2,1,0:T(1,128)} %psum.21), calls=%async_computation.4 | async-start | bytes 16384 | tf_op jit(solution)/shard_map/all_to_all | solution.py:221
  209.3 4.8 %fusion.5 = f32[768,2048]{1,0:T(8,128)S(1)} fusion(bf16[1,2048,512]{2,1,0:T(8,128)(2,1)S(1)} %copy-done, f32[768,512]{0,1:T(8,128)} %fusion.7, f32[768,512]{0,1:T(8,128)} %get-tuple-element.25, f32[768,512]{0,1:T(8,128)} %fusion.10), kind=kOutput, calls=%fused_computation.17 | convolution fusion | flops 1614544896 | bytes 13107200 | tf_op jit(solution)/shard_map/esh,edh->esd/dot_general | solution.py:214
  214.1 3.6 %add_convert_fusion = bf16[768,2048]{1,0:T(8,128)(2,1)} fusion(f32[768,2048]{1,0:T(8,128)S(1)} %fusion.5, bf16[1,2048,512]{2,1,0:T(8,128)(2,1)S(1)} %copy-done.8, f32[768,512]{0,1:T(8,128)S(1)} %copy-done.11, f32[768,512]{0,1:T(8,128)S(1)} %copy-done.9), kind=kOutput, calls=%fused_computation.5 | convolution fusion | flops 1616117760 | bytes 14680064 | tf_op jit(solution)/shard_map/esh,edh->esd/dot_general | solution.py:215
  217.7 7.0 %all-to-all-start.2 = ((bf16[16,48,2048]{2,1,0:T(8,128)(2,1)}), bf16[16,48,2048]{2,1,0:T(8,128)(2,1)S(1)}, u32[]{:S(2)}, u32[]{:S(2)}) async-start(bf16[16,48,2048]{2,1,0:T(8,128)(2,1)} %bitcast.89), calls=%async_computation.2 | async-start | bytes 6291456 | tf_op jit(solution)/shard_map/all_to_all | solution.py:218
  224.8 1.9 all_gather.27
  226.7 2.7 fusion.22
  229.4 0.5 broadcast.185
  229.9 0.7 reduce.12
  230.7 2.3 gather_fusion.1
  233.0 0.1 reshape.255
  233.3 2.5 fusion.26
  235.9 52.8 %all-to-all-done.2 = bf16[16,48,2048]{2,1,0:T(8,128)(2,1)S(1)} async-done(((bf16[16,48,2048]{2,1,0:T(8,128)(2,1)}), bf16[16,48,2048]{2,1,0:T(8,128)(2,1)S(1)}, u32[]{:S(2)}, u32[]{:S(2)}) %all-to-all-start.2) | async-done | bytes 3145760 | tf_op jit(solution)/shard_map/all_to_all | solution.py:218
  288.7 1.7 copy-done.2
  290.4 0.1 copy.42
  290.6 0.1 reshape.296
  290.7 3.8 %scatter_custom_fusion.2 = bf16[768]{0:T(1024)(128)(2,1)S(1)} fusion(s32[512]{0:T(512)S(1)} %bitcast.100, bf16[512]{0:T(512)(128)(2,1)S(1)} %reshape.296, bf16[]{:T(256)} %constant.21.clone.1), kind=kCustom, calls=%fused_computation.82 | custom fusion | bytes 1538 | tf_op jit(solution)/shard_map/scatter | solution.py:57
  294.5 0.7 all_to_all.28
  295.2 16.0 %all-to-all-start.4 = ((bf16[16,1,48]{2,1,0:T(2,128)(2,1)}), bf16[16,1,48]{2,1,0:T(2,128)(2,1)S(1)}, u32[]{:S(2)}, u32[]{:S(2)}) async-start(bf16[16,1,48]{2,1,0:T(2,128)(2,1)} %all_to_all.28), calls=%async_computation.5 | async-start | bytes 16384 | tf_op jit(solution)/shard_map/all_to_all | solution.py:199
  311.2 7.2 %all-to-all-done.4 = bf16[16,1,48]{2,1,0:T(2,128)(2,1)S(1)} async-done(((bf16[16,1,48]{2,1,0:T(2,128)(2,1)}), bf16[16,1,48]{2,1,0:T(2,128)(2,1)S(1)}, u32[]{:S(2)}, u32[]{:S(2)}) %all-to-all-start.4) | async-done | bytes 1568 | tf_op jit(solution)/shard_map/all_to_all | solution.py:199
  318.5 7.2 %fusion.2 = bf16[1,512,2048]{2,1,0:T(8,128)(2,1)} fusion(bf16[768,2048]{1,0:T(8,128)(2,1)} %bitcast.8, f32[768]{0:T(1024)S(1)} %reshape.259, f32[768,512]{0,1:T(8,128)} %fusion.10, f32[768,512]{0,1:T(8,128)} %fusion.7), kind=kOutput, calls=%fused_computation.14 | convolution fusion | flops 1614413824 | bytes 8391680 | tf_op jit(solution)/shard_map/esh,esd->ehd/dot_general | solution.py:86
  325.7 5.3 %fusion.1 = bf16[1,2048,512]{2,1,0:T(8,128)(2,1)} fusion(bf16[768,2048]{1,0:T(8,128)(2,1)} %bitcast.11, f32[768]{0:T(1024)S(1)} %reshape.259, f32[768,512]{0,1:T(8,128)S(1)} %copy-done.12, f32[768,512]{0,1:T(8,128)S(1)} %copy-done.10), kind=kOutput, calls=%fused_computation.13 | convolution fusion | flops 1614413824 | bytes 8391680 | tf_op jit(solution)/shard_map/esd,esh->edh/dot_general | solution.py:83
  331.0 5.2 %fusion = bf16[1,2048,512]{2,1,0:T(8,128)(2,1)} fusion(bf16[768,2048]{1,0:T(8,128)(2,1)} %bitcast.11, f32[768]{0:T(1024)S(1)} %reshape.259, f32[768,512]{0,1:T(8,128)S(1)} %copy-done.10, f32[768,512]{0,1:T(8,128)S(1)} %copy-done.12, f32[768,512]{0,1:T(8,128)S(1)} %copy-done.13), kind=kOutput, calls=%fused_computation.12 | convolution fusion | flops 1615986688 | bytes 9964544 | tf_op jit(solution)/shard_map/esd,esh->edh/dot_general | solution.py:80
  336.2 1.8 copy.47
  338.0 0.8 bitcast_reduce_fusion
  338.8 1.8 convert_element_type.108
  340.6 2.7 gather_fusion
  343.3 2.5 reshape.253
  345.9 1.6 fusion.49
  347.5 1.5 fusion.47
  349.0 2.5 all-reduce
  351.5 2.5 add_convert_fusion.1
  (59 shorter events, 0.8 us)
Async XLA Ops:
  7.2 117.6 %copy-start = (bf16[1,2048,512]{2,1,0:T(8,128)(2,1)S(1)}, bf16[1,2048,512]{2,1,0:T(8,128)(2,1)}, u32[]{:S(2)}) copy-start(bf16[1,2048,512]{2,1,0:T(8,128)(2,1)} %param.17) | copy-start | bytes 6291460
  7.2 14.1 %all-gather.5.cloned.1.call-start = ((), (), s32[]{:S(2)}) async-start(), calls=%async_computation.6 | async-start | bytes 1572864 | tf_op jit(solution)/shard_map/all_gather | solution.py:159
  40.2 7.7 %copy-start.6 = (bf16[1,1024]{1,0:T(2,128)(2,1)S(1)}, bf16[1,1024]{1,0:T(2,128)(2,1)}, u32[]{:S(2)}) copy-start(bf16[1,1024]{1,0:T(2,128)(2,1)} %param.16) | copy-start | bytes 6148
  40.2 68.3 %all-to-all-start.1 = ((bf16[16,48,2048]{2,1,0:T(8,128)(2,1)}), bf16[16,48,2048]{2,1,0:T(8,128)(2,1)}, u32[]{:S(2)}, u32[]{:S(2)}) async-start(bf16[16,48,2048]{2,1,0:T(8,128)(2,1)} %bitcast.87), calls=%async_computation.1 | async-start | bytes 6291456 | tf_op jit(solution)/shard_map/all_to_all | solution.py:185
  47.2 12.7 %all-gather.7.cloned.1.call-start = ((), (), s32[]{:S(2)}) async-start(), calls=%async_computation.7 | async-start | bytes 1572864 | tf_op jit(solution)/shard_map/all_gather | solution.py:160
  108.5 76.9 %all-to-all-start = ((bf16[16,48,2048]{2,1,0:T(8,128)(2,1)}), bf16[16,48,2048]{2,1,0:T(8,128)(2,1)}, u32[]{:S(2)}, u32[]{:S(2)}) async-start(bf16[16,48,2048]{2,1,0:T(8,128)(2,1)} %bitcast.88), calls=%async_computation | async-start | bytes 6291456 | tf_op jit(solution)/shard_map/all_to_all | solution.py:192
  124.8 5.0 %copy-start.7 = (bf16[1,2048,512]{2,1,0:T(8,128)(2,1)S(1)}, bf16[1,2048,512]{2,1,0:T(8,128)(2,1)}, u32[]{:S(2)}) copy-start(bf16[1,2048,512]{2,1,0:T(8,128)(2,1)} %param.18) | copy-start | bytes 6291460
  195.1 22.6 %all-to-all-start.3 = ((f32[16,1,48]{2,1,0:T(1,128)}), f32[16,1,48]{2,1,0:T(1,128)S(1)}, u32[]{:S(2)}, u32[]{:S(2)}) async-start(f32[16,1,48]{2,1,0:T(1,128)} %psum.21), calls=%async_computation.4 | async-start | bytes 16384 | tf_op jit(solution)/shard_map/all_to_all | solution.py:221
  209.2 4.8 %copy-start.8 = (bf16[1,2048,512]{2,1,0:T(8,128)(2,1)S(1)}, bf16[1,2048,512]{2,1,0:T(8,128)(2,1)}, u32[]{:S(2)}) copy-start(bf16[1,2048,512]{2,1,0:T(8,128)(2,1)} %param.18) | copy-start | bytes 6291460
  209.3 4.8 %copy-start.9 = (f32[768,512]{0,1:T(8,128)S(1)}, f32[768,512]{0,1:T(8,128)}, u32[]{:S(2)}) copy-start(f32[768,512]{0,1:T(8,128)} %fusion.7) | copy-start | bytes 4718596
  209.3 4.8 %copy-start.11 = (f32[768,512]{0,1:T(8,128)S(1)}, f32[768,512]{0,1:T(8,128)}, u32[]{:S(2)}) copy-start(f32[768,512]{0,1:T(8,128)} %get-tuple-element.25) | copy-start | bytes 4718596
  217.7 7.1 %copy-start.4 = (f32[1024,16]{0,1:T(8,128)S(1)}, f32[1024,16]{0,1:T(8,128)}, u32[]{:S(2)}) copy-start(f32[1024,16]{0,1:T(8,128)} %param.13) | copy-start | bytes 196612
  217.7 71.0 %all-to-all-start.2 = ((bf16[16,48,2048]{2,1,0:T(8,128)(2,1)}), bf16[16,48,2048]{2,1,0:T(8,128)(2,1)S(1)}, u32[]{:S(2)}, u32[]{:S(2)}) async-start(bf16[16,48,2048]{2,1,0:T(8,128)(2,1)} %bitcast.89), calls=%async_computation.2 | async-start | bytes 6291456 | tf_op jit(solution)/shard_map/all_to_all | solution.py:218
  224.7 4.6 %copy-start.5 = (s32[256,2]{0,1:T(2,128)S(1)}, s32[256,2]{0,1:T(2,128)}, u32[]{:S(2)}) copy-start(s32[256,2]{0,1:T(2,128)} %param.12) | copy-start | bytes 6148
  224.8 111.4 %all-gather.9.cloned.1.call-start = ((), (), s32[]{:S(2)}) async-start(), calls=%async_computation.9 | async-start | bytes 1114112 | tf_op jit(solution)/shard_map/all_gather | solution.py:120
  235.8 103.0 %reduce-scatter.2.cloned.1.call-start = ((), (), s32[]{:S(2)}) async-start(), calls=%async_computation.8 | async-start | bytes 4718592 | tf_op jit(solution)/shard_map/reduce_scatter | solution.py:224
  288.7 1.7 copy-start.2
  295.2 23.3 %all-to-all-start.4 = ((bf16[16,1,48]{2,1,0:T(2,128)(2,1)}), bf16[16,1,48]{2,1,0:T(2,128)(2,1)S(1)}, u32[]{:S(2)}, u32[]{:S(2)}) async-start(bf16[16,1,48]{2,1,0:T(2,128)(2,1)} %all_to_all.28), calls=%async_computation.5 | async-start | bytes 16384 | tf_op jit(solution)/shard_map/all_to_all | solution.py:199
  318.5 7.2 %copy-start.10 = (f32[768,512]{0,1:T(8,128)S(1)}, f32[768,512]{0,1:T(8,128)}, u32[]{:S(2)}) copy-start(f32[768,512]{0,1:T(8,128)} %fusion.7) | copy-start | bytes 4718596
  318.5 7.2 %copy-start.12 = (f32[768,512]{0,1:T(8,128)S(1)}, f32[768,512]{0,1:T(8,128)}, u32[]{:S(2)}) copy-start(f32[768,512]{0,1:T(8,128)} %get-tuple-element.25) | copy-start | bytes 4718596
  325.7 5.3 %copy-start.13 = (f32[768,512]{0,1:T(8,128)S(1)}, f32[768,512]{0,1:T(8,128)}, u32[]{:S(2)}) copy-start(f32[768,512]{0,1:T(8,128)} %fusion.10) | copy-start | bytes 4718596
  345.8 1.6 copy-start.3
  347.5 6.5 %copy-start.1 = (bf16[1,2048,512]{2,1,0:T(8,128)(2,1)S(1)}, bf16[1,2048,512]{2,1,0:T(8,128)(2,1)}, u32[]{:S(2)}) copy-start(bf16[1,2048,512]{2,1,0:T(8,128)(2,1)} %param.17) | copy-start | bytes 6291460
Sparse Core Ops, SparseCore 0:
  9.5 11.7 all-gather.4
  49.6 10.2 all-gather.6
  235.9 76.7 all-gather.8
  314.8 9.7 reduce-scatter.1
